TPU v7x, 512 devices: a whole 4x8x8 slice. The times are simulated.
512 devices in a mesh: dp: 8 (over z), expert: 64 (over y, x, core).
Axes of the slice: x: 4, y: 8, z: 8, core: 2. Of those that a mesh axis runs over, the one named last changes fastest.
Arguments:
- inputs: bfloat16 [8, 64, 256, 256], P('dp', 'expert'), may hold values from -6 to 6
- layer_weights: bfloat16 [64, 8, 256, 256], P('expert'), may hold values from -0.375 to 0.375
- layer_biases: float32 [64, 8, 256], P('expert'), may hold values from -3 to 3
- head_weight: bfloat16 [4, 256], replicated, may hold values from -0.375 to 0.375
- head_bias: float32 [4], replicated, may hold values from -3 to 3
- gate_values: float32 [8, 64, 256], P('dp', 'expert'), may hold values from 0.3 to 1
- spacing: float32 [8, 64, 256], P('dp', 'expert'), may hold values from 0.004 to 0.04
- ray_index: int32 [8, 64, 256], P('dp', 'expert'), may hold values from 0 to 3, never falling along the last dimension, each value on 1 to 96 neighbouring positions
- expert_index: int32 [8, 64, 256], P('dp', 'expert'), may hold values from 0 to 63, as said below
- slot_index: int32 [8, 64, 256], P('dp', 'expert'), may hold values from 0 to 7, as said below
- color_cotangent: float32 [8, 64, 3, 4], P('dp', 'expert'), may hold values from -6 to 6
Outputs:
- grad_inputs: bfloat16 [8, 64, 256, 256], P('dp', 'expert')
- grad_weights: float32 [64, 8, 256, 256], P('expert')
- grad_biases: float32 [64, 8, 256], P('expert')
- grad_head_weight: float32 [4, 256], replicated
- grad_head_bias: float32 [4], replicated
Inputs may be any that keep to these rules, and one draw needn't show every extreme that they name: `expert_index`: on each device, at most 8 samples name one expert; one expert, the same on every device, is named by exactly 8 samples on every device. `slot_index`: on each device, the n samples that name one expert hold the slots 0 to n - 1, each once. `ray_index`: never falling along the samples of a device; every ray 0 to 3 holds 1 to 96 consecutive samples, and some ray exactly 96.
All inputs are finite; a program needn't handle non-finite values.
Results may differ from a plain program's by a relative error of at most 0.02.
Values may be sent and summed in bfloat16 or wider, within the bound.
A program may use at most 64 MiB of HBM per device.

v0:
```python
import jax
import jax.numpy as jnp
from jax import lax
from jax.sharding import PartitionSpec as P


def forward(rows, weights, biases):
    layers = weights.shape[0]
    activations = [rows]
    current = rows
    outcome = None
    for number in range(layers):
        summed = (
            jnp.dot(current, weights[number], preferred_element_type=jnp.float32) + biases[number]
        )
        if number < layers - 1:
            current = jax.nn.softplus(summed).astype(jnp.bfloat16)
            activations.append(current)
        else:
            outcome = summed.astype(jnp.bfloat16)
    return (activations, outcome)


def composite_grads(sigma, colors, spacing, ray_index, cotangent):
    ray_count = cotangent.shape[1]
    count = ray_index.shape[0]
    ray_numbers = jnp.arange(ray_count, dtype=jnp.int32)
    onehot = (ray_index[:, None] == ray_numbers[None, :]).astype(jnp.float32)
    positions = jnp.arange(count, dtype=jnp.int32)
    earlier = (
        (positions[:, None] < positions[None, :]) & (ray_index[:, None] == ray_index[None, :])
    ).astype(jnp.float32)

    def render(density, shades):
        depth = density * spacing
        inside = jnp.dot(depth, earlier, precision=lax.Precision.HIGHEST)
        weight = jnp.exp(-inside) * -jnp.expm1(-depth)
        return jnp.dot(shades * weight[None, :], onehot, precision=lax.Precision.HIGHEST)

    _, pullback = jax.vjp(render, sigma, colors)
    return pullback(cotangent)


def head_backward(unscaled, gates, head_bias, spacing, ray_index, cotangent):
    logits = gates[:, None] * unscaled + head_bias[None, :]
    sigma = jax.nn.softplus(logits[:, 0])
    colors = jax.nn.sigmoid(logits[:, 1:])
    grad_sigma, grad_colors = composite_grads(sigma, colors.T, spacing, ray_index, cotangent)
    first = grad_sigma * jax.nn.sigmoid(logits[:, 0])
    others = grad_colors.T * colors * (1.0 - colors)
    return jnp.concatenate([first[:, None], others], axis=1)


def per_device(
    inputs,
    layer_weights,
    layer_biases,
    head_weight,
    head_bias,
    gate_values,
    spacing,
    ray_index,
    expert_index,
    slot_index,
    color_cotangent,
):
    samples = inputs.shape[2]
    width = inputs.shape[3]
    experts = lax.axis_size("expert")
    capacity = 2 * samples // experts
    slot_total = experts * capacity
    layers = layer_weights.shape[1]
    rows_local = inputs.reshape(samples, width)
    cell_index = (expert_index * capacity + slot_index).reshape(samples)
    send_rows = jnp.zeros((slot_total, width), jnp.bfloat16).at[cell_index].set(rows_local)
    received = lax.all_to_all(
        send_rows.reshape(experts, capacity, width),
        "expert",
        split_axis=0,
        concat_axis=0,
        tiled=True,
    )
    expert_rows = received.reshape(slot_total, width)
    weights = layer_weights[0]
    biases = layer_biases[0]
    activations, features = forward(expert_rows, weights, biases)
    head_float = head_weight.astype(jnp.float32)
    gates = gate_values.reshape(samples)
    returned = lax.all_to_all(
        features.reshape(experts, capacity, width),
        "expert",
        split_axis=0,
        concat_axis=0,
        tiled=True,
    )
    features_mine = returned.reshape(slot_total, width)[cell_index]
    unscaled = lax.dot_general(
        features_mine, head_weight, (((1,), (1,)), ((), ())), preferred_element_type=jnp.float32
    )
    grad_logits = head_backward(
        unscaled,
        gates,
        head_bias,
        spacing.reshape(samples),
        ray_index.reshape(samples),
        color_cotangent.reshape(3, color_cotangent.shape[3]),
    )
    scaled = gates[:, None] * grad_logits
    head_part = lax.dot_general(
        scaled,
        features_mine.astype(jnp.float32),
        (((0,), (0,)), ((), ())),
        precision=lax.Precision.HIGHEST,
    )
    grads_mine = jnp.dot(scaled, head_float, precision=lax.Precision.HIGHEST).astype(jnp.bfloat16)
    send_grads = jnp.zeros((slot_total, width), jnp.bfloat16).at[cell_index].set(grads_mine)
    upstream = lax.all_to_all(
        send_grads.reshape(experts, capacity, width),
        "expert",
        split_axis=0,
        concat_axis=0,
        tiled=True,
    ).reshape(slot_total, width)
    bias_part = jnp.sum(grad_logits, axis=0)
    grad_head_weight, grad_head_bias = lax.psum((head_part, bias_part), ("dp", "expert"))
    weight_grads = [None] * layers
    bias_grads = [None] * layers
    input_slots = None
    for number in reversed(range(layers)):
        weight_term = lax.dot_general(
            activations[number],
            upstream,
            (((0,), (0,)), ((), ())),
            preferred_element_type=jnp.float32,
        )
        bias_term = jnp.sum(upstream.astype(jnp.float32), axis=0)
        spread = lax.dot_general(
            upstream, weights[number], (((1,), (1,)), ((), ())), preferred_element_type=jnp.float32
        )
        weight_grads[number] = weight_term
        bias_grads[number] = bias_term
        if number > 0:
            slope = -jnp.expm1(-activations[number].astype(jnp.float32))
            upstream = (spread * slope).astype(jnp.bfloat16)
        else:
            input_slots = spread.astype(jnp.bfloat16)
    stacked_weights = jnp.stack(weight_grads)
    stacked_biases = jnp.stack(bias_grads)
    stacked_weights, stacked_biases = lax.psum((stacked_weights, stacked_biases), "dp")
    returned_grads = lax.all_to_all(
        input_slots.reshape(experts, capacity, width),
        "expert",
        split_axis=0,
        concat_axis=0,
        tiled=True,
    )
    grad_inputs = returned_grads.reshape(slot_total, width)[cell_index].reshape(
        1, 1, samples, width
    )
    return (
        grad_inputs,
        stacked_weights[None],
        stacked_biases[None],
        grad_head_weight,
        grad_head_bias,
    )


def solution(mesh):
    in_specs = (
        P("dp", "expert", None, None),
        P("expert", None, None, None),
        P("expert", None, None),
        P(),
        P(),
        P("dp", "expert", None),
        P("dp", "expert", None),
        P("dp", "expert", None),
        P("dp", "expert", None),
        P("dp", "expert", None),
        P("dp", "expert", None, None),
    )
    out_specs = (
        P("dp", "expert", None, None),
        P("expert", None, None, None),
        P("expert", None, None),
        P(),
        P(),
    )
    return jax.shard_map(
        per_device, mesh=mesh, in_specs=in_specs, out_specs=out_specs, check_vma=False
    )
```

profile of v0, /device:TPU:2, one launch (start us, length us, event | category | flops | bytes accessed | tf_op | source)
XLA Modules:
  0.0 231.4 jit_solution(11086977512699708950)
XLA Ops:
  7.2 0.8 compare_select_fusion.7
  8.1 2.1 scatter_custom_fusion
  10.2 10.7 %all-to-all-start = ((bf16[64,8,256]{2,1,0:T(8,128)(2,1)}), bf16[64,8,256]{2,1,0:T(8,128)(2,1)S(1)}, u32[]{:S(2)}, u32[]{:S(2)}) async-start(bf16[64,8,256]{2,1,0:T(8,128)(2,1)} %bitcast.4), calls=%async_computation | async-start | bytes 524288 | tf_op jit(solution)/shard_map/all_to_all | solution.py:76
  20.9 1.0 fusion.93
  21.9 11.2 %all-to-all-done = bf16[64,8,256]{2,1,0:T(8,128)(2,1)S(1)} async-done(((bf16[64,8,256]{2,1,0:T(8,128)(2,1)}), bf16[64,8,256]{2,1,0:T(8,128)(2,1)S(1)}, u32[]{:S(2)}, u32[]{:S(2)}) %all-to-all-start) | async-done | bytes 262176 | tf_op jit(solution)/shard_map/all_to_all | solution.py:76
  33.1 1.4 fusion.19
  34.5 0.5 fusion.20
  36.9 1.5 fusion.25
  38.4 1.8 fusion.8
  40.2 5.6 %all-to-all-start.1 = ((bf16[64,8,256]{2,1,0:T(8,128)(2,1)}), bf16[64,8,256]{2,1,0:T(8,128)(2,1)S(1)}, u32[]{:S(2)}, u32[]{:S(2)}) async-start(bf16[64,8,256]{2,1,0:T(8,128)(2,1)} %fusion.8), calls=%async_computation.1 | async-start | bytes 524288 | tf_op jit(solution)/shard_map/all_to_all | solution.py:89
  46.0 12.1 %all-to-all-done.1 = bf16[64,8,256]{2,1,0:T(8,128)(2,1)S(1)} async-done(((bf16[64,8,256]{2,1,0:T(8,128)(2,1)}), bf16[64,8,256]{2,1,0:T(8,128)(2,1)S(1)}, u32[]{:S(2)}, u32[]{:S(2)}) %all-to-all-start.1) | async-done | bytes 262176 | tf_op jit(solution)/shard_map/all_to_all | solution.py:89
  58.1 1.2 gather_fusion
  60.8 1.5 scatter_custom_fusion.1
  62.3 17.8 %all_to_all.20 = bf16[64,8,256]{2,1,0:T(8,128)(2,1)S(1)} all-to-all(bf16[64,8,256]{2,1,0:T(8,128)(2,1)S(1)} %bitcast.184), channel_id=1, replica_groups=mesh['dp'=8,'expert'=64] {'expert'}, dimensions={0} | all-to-all | bytes 524288 | tf_op jit(solution)/shard_map/all_to_all | solution.py:117
  80.1 1.3 convert_reduce_fusion.1
  81.4 1.3 convert_reduce_fusion.2
  84.9 1.3 fusion.16
  88.0 1.3 copy-done.1
  89.3 1.9 fusion.9
  91.2 5.6 %all-to-all-start.3 = ((bf16[64,8,256]{2,1,0:T(8,128)(2,1)}), bf16[64,8,256]{2,1,0:T(8,128)(2,1)S(1)}, u32[]{:S(2)}, u32[]{:S(2)}) async-start(bf16[64,8,256]{2,1,0:T(8,128)(2,1)} %fusion.9), calls=%async_computation.3 | async-start | bytes 524288 | tf_op jit(solution)/shard_map/all_to_all | solution.py:150
  97.1 106.2 %all-reduce = (f32[4,256]{1,0:T(4,128)}, f32[4]{0:T(128)}) all-reduce(f32[4,256]{1,0:T(4,128)S(1)} %fusion.81, f32[4]{0:T(128)S(1)} %fusion.90), channel_id=1, replica_groups=mesh['dp'=8,'expert'=64] {'dp','expert'}, use_global_device_ids=true, to_apply=%region_13.14 | all-reduce | flops 1028 | bytes 8224 | tf_op jit(solution)/shard_map/psum | solution.py:125
  203.4 16.3 %psum.29 = f32[1,8,256]{2,1,0:T(8,128)} all-reduce(f32[1,8,256]{2,1,0:T(8,128)S(1)} %bitcast.186), channel_id=1, replica_groups=mesh['dp'=8,'expert'=64] {'dp'}, use_global_device_ids=true, to_apply=%region_12.13 | all-reduce | flops 2048 | bytes 16384 | tf_op jit(solution)/shard_map/psum | solution.py:149
  219.7 1.8 gather_fusion.1
  221.5 3.0 %copy.31 = f32[1,8,256,256]{3,2,1,0:T(8,128)} copy(f32[1,8,256,256]{3,2,1,0:T(8,128)} %all-reduce.3.cloned.1.call-done) | data formatting | bytes 4194304
  (76 shorter events, 7.7 us)
Async XLA Ops:
  7.2 27.3 %copy-start.13 = (bf16[1,8,256,256]{3,2,1,0:T(8,128)(2,1)S(1)}, bf16[1,8,256,256]{3,2,1,0:T(8,128)(2,1)}, u32[]{:S(2)}) copy-start(bf16[1,8,256,256]{3,2,1,0:T(8,128)(2,1)} %param.12) | copy-start | bytes 3145732
  10.2 22.9 %all-to-all-start = ((bf16[64,8,256]{2,1,0:T(8,128)(2,1)}), bf16[64,8,256]{2,1,0:T(8,128)(2,1)S(1)}, u32[]{:S(2)}, u32[]{:S(2)}) async-start(bf16[64,8,256]{2,1,0:T(8,128)(2,1)} %bitcast.4), calls=%async_computation | async-start | bytes 524288 | tf_op jit(solution)/shard_map/all_to_all | solution.py:76
  34.4 49.8 %copy-start.12 = (bf16[512,256]{1,0:T(8,128)(2,1)}, bf16[512,256]{1,0:T(8,128)(2,1)S(1)}, u32[]{:S(2)}) copy-start(bf16[512,256]{1,0:T(8,128)(2,1)S(1)} %fusion.19) | copy-start | bytes 786436
  34.9 48.9 %copy-start.10 = (bf16[512,256]{1,0:T(8,128)(2,1)}, bf16[512,256]{1,0:T(8,128)(2,1)S(1)}, u32[]{:S(2)}) copy-start(bf16[512,256]{1,0:T(8,128)(2,1)S(1)} %fusion.20) | copy-start | bytes 786436
  35.4 48.1 %copy-start.8 = (bf16[512,256]{1,0:T(8,128)(2,1)}, bf16[512,256]{1,0:T(8,128)(2,1)S(1)}, u32[]{:S(2)}) copy-start(bf16[512,256]{1,0:T(8,128)(2,1)S(1)} %fusion.21) | copy-start | bytes 786436
  35.9 47.2 %copy-start.6 = (bf16[512,256]{1,0:T(8,128)(2,1)}, bf16[512,256]{1,0:T(8,128)(2,1)S(1)}, u32[]{:S(2)}) copy-start(bf16[512,256]{1,0:T(8,128)(2,1)S(1)} %fusion.22) | copy-start | bytes 786436
  36.4 46.3 %copy-start.4 = (bf16[512,256]{1,0:T(8,128)(2,1)}, bf16[512,256]{1,0:T(8,128)(2,1)S(1)}, u32[]{:S(2)}) copy-start(bf16[512,256]{1,0:T(8,128)(2,1)S(1)} %fusion.23) | copy-start | bytes 786436
  36.8 44.6 %copy-start.2 = (bf16[512,256]{1,0:T(8,128)(2,1)}, bf16[512,256]{1,0:T(8,128)(2,1)S(1)}, u32[]{:S(2)}) copy-start(bf16[512,256]{1,0:T(8,128)(2,1)S(1)} %fusion.24) | copy-start | bytes 786436
  36.8 22.4 %copy-start.15 = (f32[1,1,256]{2,1,0:T(1,128)S(1)}, f32[1,1,256]{2,1,0:T(1,128)}, u32[]{:S(2)}) copy-start(f32[1,1,256]{2,1,0:T(1,128)} %param.16) | copy-start | bytes 3076
  36.8 22.4 %copy-start.17 = (bf16[4,256]{1,0:T(4,128)(2,1)S(1)}, bf16[4,256]{1,0:T(4,128)(2,1)}, u32[]{:S(2)}) copy-start(bf16[4,256]{1,0:T(4,128)(2,1)} %param.14) | copy-start | bytes 6148
  36.9 22.4 %copy-start.20 = (f32[4]{0:T(128)S(1)}, f32[4]{0:T(128)}, u32[]{:S(2)}) copy-start(f32[4]{0:T(128)} %param.15) | copy-start | bytes 52
  36.9 22.6 %copy-start.16 = (f32[1,1,256]{2,1,0:T(1,128)S(1)}, f32[1,1,256]{2,1,0:T(1,128)}, u32[]{:S(2)}) copy-start(f32[1,1,256]{2,1,0:T(1,128)} %param.17) | copy-start | bytes 3076
  36.9 22.6 %copy-start.19 = (s32[1,1,256]{2,1,0:T(1,128)S(1)}, s32[1,1,256]{2,1,0:T(1,128)}, u32[]{:S(2)}) copy-start(s32[1,1,256]{2,1,0:T(1,128)} %param.18) | copy-start | bytes 3076
  36.9 22.9 %copy-start.18 = (f32[1,1,3,4]{3,1,2,0:T(1,128)S(1)}, f32[1,1,3,4]{3,1,2,0:T(1,128)}, u32[]{:S(2)}) copy-start(f32[1,1,3,4]{3,1,2,0:T(1,128)} %param.21) | copy-start | bytes 148
  40.2 17.9 %all-to-all-start.1 = ((bf16[64,8,256]{2,1,0:T(8,128)(2,1)}), bf16[64,8,256]{2,1,0:T(8,128)(2,1)S(1)}, u32[]{:S(2)}, u32[]{:S(2)}) async-start(bf16[64,8,256]{2,1,0:T(8,128)(2,1)} %fusion.8), calls=%async_computation.1 | async-start | bytes 524288 | tf_op jit(solution)/shard_map/all_to_all | solution.py:89
  45.9 175.6 %all-reduce.3.cloned.1.call-start = ((), (), s32[]{:S(2)}) async-start(), calls=%async_computation.4 | async-start | bytes 4194304 | tf_op jit(solution)/shard_map/psum | solution.py:149
  62.3 20.4 %copy-start.14 = (bf16[1,8,256,256]{3,2,1,0:T(8,128)(2,1)S(1)}, bf16[1,8,256,256]{3,2,1,0:T(8,128)(2,1)}, u32[]{:S(2)}) copy-start(bf16[1,8,256,256]{3,2,1,0:T(8,128)(2,1)} %param.12) | copy-start | bytes 3145732
  84.2 2.0 copy-start.11
  84.2 2.3 copy-start.9
  84.3 2.5 %copy-start.7 = (bf16[512,256]{1,0:T(8,128)(2,1)S(1)}, bf16[512,256]{1,0:T(8,128)(2,1)}, u32[]{:S(2)}) copy-start(bf16[512,256]{1,0:T(8,128)(2,1)} %copy-done.6) | copy-start | bytes 786436
  84.7 2.4 %copy-start.5 = (bf16[512,256]{1,0:T(8,128)(2,1)S(1)}, bf16[512,256]{1,0:T(8,128)(2,1)}, u32[]{:S(2)}) copy-start(bf16[512,256]{1,0:T(8,128)(2,1)} %copy-done.4) | copy-start | bytes 786436
  84.9 2.4 %copy-start.3 = (bf16[512,256]{1,0:T(8,128)(2,1)S(1)}, bf16[512,256]{1,0:T(8,128)(2,1)}, u32[]{:S(2)}) copy-start(bf16[512,256]{1,0:T(8,128)(2,1)} %copy-done.2) | copy-start | bytes 786436
  87.9 1.3 copy-start.1
  91.2 128.5 %all-to-all-start.3 = ((bf16[64,8,256]{2,1,0:T(8,128)(2,1)}), bf16[64,8,256]{2,1,0:T(8,128)(2,1)S(1)}, u32[]{:S(2)}, u32[]{:S(2)}) async-start(bf16[64,8,256]{2,1,0:T(8,128)(2,1)} %fusion.9), calls=%async_computation.3 | async-start | bytes 524288 | tf_op jit(solution)/shard_map/all_to_all | solution.py:150
  (1 other events, 0.9 us)
Sparse Core Ops, SparseCore 0:
  89.4 88.2 all-reduce.2
where the time goes:
time: 232 us; the launch traced here: 231 us
  blocking collectives  140 us (60%)
  waiting for transfers between devices  23.3 us (10%)
  starting transfers between devices  22 us (9%)
  matrix products  17.8 us (8%)
  between operations  14.5 us (6%)
  local copies, waits for them, and re-layouts  12.2 us (5%)
    psum x1, blocking collectives, per_device(): lax.psum((head_part, bias_part), ('dp', 'expert'))  106 us
    all_to_all x1, blocking collectives, per_device(): lax.all_to_all(send_grads.reshape(experts, capacity, width), 'expert', sp...  17.8 us
    psum x1, blocking collectives, per_device(): lax.psum((stacked_weights, stacked_biases), 'dp')  16.3 us
    all_to_all x1, waiting for transfers between devices, per_device(): lax.all_to_all(features.reshape(experts, capacity, width), 'expert', spli...  12.1 us
    all_to_all x1, waiting for transfers between devices, per_device(): lax.all_to_all(send_rows.reshape(experts, capacity, width), 'expert', spl...  11.2 us
    all_to_all x1, starting transfers between devices, per_device(): lax.all_to_all(send_rows.reshape(experts, capacity, width), 'expert', spl...  10.7 us
    dot_general x8, matrix products, forward(): jnp.dot(current, weights[number], preferred_element_type=jnp.float32)  6.99 us
    dot_general x8, matrix products, per_device(): lax.dot_general(upstream, weights[number], (((1,), (1,)), ((), ())), pref...  6.33 us
  transfers between devices with their start and end apart: 4, of which 2 were waited for; matrix products, arithmetic and copies ran while one was open for 2% of the time, Pallas kernels for 0%

commit v1 on v0

v1 whole, which is shorter than its diff:
```python
import functools

import jax
import jax.numpy as jnp
from jax import lax
from jax.experimental import pallas as pl
from jax.experimental.pallas import tpu as pltpu
from jax.sharding import PartitionSpec as P

MESH = pl.DeviceIdType.MESH
HIGHEST = lax.Precision.HIGHEST
F32 = jnp.float32
BF16 = jnp.bfloat16


def matmul(a, b, dims, precision=None):
    return lax.dot_general(
        a, b, (dims, ((), ())), precision=precision, preferred_element_type=F32
    )


def softplus(v):
    return jnp.maximum(v, 0.0) + jnp.log1p(jnp.exp(-jnp.abs(v)))


def sigmoid(v):
    small = jnp.exp(-jnp.abs(v))
    return jnp.where(v >= 0.0, 1.0, small) / (1.0 + small)


def one_minus_exp(t):
    series = t * (1.0 - t * (0.5 - t * (1.0 / 6.0 - t * (1.0 / 24.0 - t * (1.0 / 120.0)))))
    return jnp.where(t < 0.06, series, 1.0 - jnp.exp(-t))


def factors(experts):
    stages = []
    stride = 1
    for extent in (2, 4, 8):
        extent = min(extent, experts // stride)
        if extent > 1:
            stages.append((extent, stride))
            stride *= extent
    return stages


def composite(unscaled, gate, hb_ref, spacing, ray, ct_ref):
    rays = ct_ref.shape[1]
    samples = ray.shape[1]
    logits = [gate * unscaled[h : h + 1, :] + hb_ref[0:1, h : h + 1] for h in range(4)]
    sigma = softplus(logits[0])
    colors = [sigmoid(logits[h]) for h in range(1, 4)]
    tau = sigma * spacing
    hot = (lax.broadcasted_iota(jnp.int32, (8, samples), 0) == ray).astype(F32)
    same = matmul(hot.astype(BF16), hot.astype(BF16), ((0,), (0,)))
    before = lax.broadcasted_iota(jnp.int32, (samples, samples), 0)
    after = lax.broadcasted_iota(jnp.int32, (samples, samples), 1)
    earlier = jnp.where(before < after, same, 0.0)
    inside = matmul(jnp.broadcast_to(tau, (8, samples)), earlier, ((1,), (0,)), HIGHEST)[0:1, :]
    clear = jnp.exp(-inside)
    opacity = one_minus_exp(tau)
    weight = clear * opacity
    grads = []
    weight_grad = jnp.zeros_like(weight)
    for k in range(3):
        cotangent = jnp.zeros_like(weight)
        for r in range(rays):
            cotangent += ct_ref[k : k + 1, r : r + 1] * hot[r : r + 1, :]
        weight_grad += cotangent * colors[k]
        grads.append(cotangent * weight * colors[k] * (1.0 - colors[k]))
    inside_grad = -weight_grad * weight
    spread = matmul(
        jnp.broadcast_to(inside_grad, (8, samples)), earlier, ((1,), (1,)), HIGHEST
    )[0:1, :]
    tau_grad = weight_grad * clear * jnp.exp(-tau) + spread
    first = tau_grad * spacing * sigmoid(logits[0])
    return [first] + grads


def body(
    replicas,
    experts,
    in_ref,
    w_ref,
    b_ref,
    hw_ref,
    hb_ref,
    gate_ref,
    spacing_ref,
    ray_ref,
    expert_ref,
    slot_ref,
    ct_ref,
    out_in,
    out_w,
    out_small,
    acts,
    head_rows,
    row_send,
    row_recv,
    up_send,
    up_recv,
    down_send,
    down_recv,
    back_send,
    back_recv,
    part,
    chain_send,
    chain_recv,
    head_part,
    head_recv,
    small,
    small_recv,
    a2a_send_sem,
    a2a_recv_sem,
    chain_send_sem,
    chain_recv_sem,
    ring_send_sem,
    ring_recv_sem,
    head_send_sem,
    head_recv_sem,
    small_send_sem,
    small_recv_sem,
):
    samples, width = in_ref.shape
    layers = w_ref.shape[0]
    cap = 2 * samples // experts
    cells = experts * cap
    lanes = head_rows.shape[0]
    piece = width // replicas
    me_d = lax.axis_index("dp")
    me_e = lax.axis_index("expert")
    above = lax.rem(me_d + 1, replicas)
    below = lax.rem(me_d + replicas - 1, replicas)
    reach = (replicas // 2, replicas - 1 - replicas // 2)
    stages = factors(experts)

    barrier = pltpu.get_barrier_semaphore()

    def greet_e(k, c):
        pl.semaphore_signal(
            barrier, inc=1, device_id={"expert": lax.rem(me_e + k, experts)}, device_id_type=MESH
        )
        return c

    def greet_d(k, c):
        pl.semaphore_signal(
            barrier, inc=1, device_id={"dp": lax.rem(me_d + k, replicas)}, device_id_type=MESH
        )
        return c

    lax.fori_loop(1, experts, greet_e, 0)
    lax.fori_loop(1, replicas, greet_d, 0)

    def exchange(phase, source, target):
        def send(k, c):
            peer = lax.rem(me_e + k, experts)
            pltpu.make_async_remote_copy(
                src_ref=source.at[peer],
                dst_ref=target.at[me_e],
                send_sem=a2a_send_sem.at[phase],
                recv_sem=a2a_recv_sem.at[phase],
                device_id={"expert": peer},
                device_id_type=MESH,
            ).start()
            return c

        lax.fori_loop(1, experts, send, 0)
        target[me_e] = source[me_e]

    def arrive(phase, source, target):
        most = pl.ds(0, experts - 1)
        pltpu.make_async_copy(source.at[most], target.at[most], a2a_recv_sem.at[phase]).wait()

    def sent(phase, source, target):
        most = pl.ds(0, experts - 1)
        pltpu.make_async_copy(source.at[most], target.at[most], a2a_send_sem.at[phase]).wait()

    cell = expert_ref[...] * cap + slot_ref[...]
    pick = (lax.broadcasted_iota(jnp.int32, (cells, samples), 0) == cell).astype(BF16)
    rows = matmul(pick, in_ref[...], ((1,), (0,)))
    row_send[...] = rows.reshape(experts, cap, width).astype(BF16)
    head_rows[...] = jnp.zeros_like(head_rows)
    for h in range(4):
        head_rows[h * cap : (h + 1) * cap, :] = jnp.broadcast_to(
            hw_ref[h : h + 1, :].astype(F32), (cap, width)
        )
    pl.semaphore_wait(barrier, experts + replicas - 2)
    exchange(0, row_send, row_recv)
    arrive(0, row_send, row_recv)
    acts[0] = row_recv[...].astype(F32).reshape(cells, width).astype(BF16)

    def forward(layer, c):
        v = matmul(acts[layer], w_ref[layer], ((1,), (0,))) + b_ref[pl.ds(layer, 1), :]
        acts[layer + 1] = softplus(v).astype(BF16)
        return c

    lax.fori_loop(0, layers - 1, forward, 0)
    features = (
        matmul(acts[layers - 1], w_ref[layers - 1], ((1,), (0,))) + b_ref[layers - 1 : layers, :]
    ).astype(BF16)
    acts[layers] = features

    own_slot = lax.broadcasted_iota(jnp.int32, (cells, lanes), 0) % cap == (
        lax.broadcasted_iota(jnp.int32, (cells, lanes), 1) % cap
    )
    product = matmul(features, head_rows[...].astype(BF16), ((1,), (1,)))
    up_send[...] = (
        jnp.where(own_slot, product, 0.0).reshape(experts, cap, lanes).sum(axis=1, keepdims=True)
    )
    exchange(1, up_send, up_recv)
    arrive(1, up_send, up_recv)

    named = (lax.broadcasted_iota(jnp.int32, (experts, samples), 0) == expert_ref[...]).astype(F32)
    table = up_recv[...].reshape(experts, lanes)
    picked = matmul(table, named, ((0,), (0,)), HIGHEST)
    slot_hot = lax.broadcasted_iota(jnp.int32, (cap, samples), 0) == slot_ref[...]
    unscaled = jnp.concatenate(
        [
            jnp.where(slot_hot, picked[h * cap : (h + 1) * cap, :], 0.0).sum(axis=0, keepdims=True)
            for h in range(4)
        ],
        axis=0,
    )
    gate = gate_ref[...]
    grad_logits = composite(unscaled, gate, hb_ref, spacing_ref[...], ray_ref[...], ct_ref)
    placed = jnp.concatenate(
        [
            jnp.where(slot_hot, jnp.broadcast_to(gate * grad_logits[h], (cap, samples)), 0.0)
            for h in range(4)
        ]
        + [jnp.zeros((lanes - 4 * cap, samples), F32)],
        axis=0,
    )
    down_send[...] = matmul(named, placed, ((1,), (1,)), HIGHEST).reshape(experts, 1, lanes)
    exchange(2, down_send, down_recv)
    for h in range(4):
        head_part[4 + h : 5 + h, :] = jnp.broadcast_to(
            grad_logits[h].sum(axis=1, keepdims=True), (1, width)
        )
    arrive(2, down_send, down_recv)

    coming = jnp.where(
        own_slot,
        jnp.broadcast_to(down_recv[...], (experts, cap, lanes)).reshape(cells, lanes),
        0.0,
    )
    first_upstream = matmul(coming, head_rows[...], ((1,), (0,)), HIGHEST).astype(BF16)
    head_all = matmul(coming, acts[layers].astype(F32), ((0,), (0,)), HIGHEST)
    for h in range(4):
        head_part[h : h + 1, :] = head_all[h * cap : (h + 1) * cap, :].sum(axis=0, keepdims=True)
    acts[layers] = first_upstream

    def head_peer(stage, k):
        extent, stride = stages[stage]
        mine = lax.rem(me_e // stride, extent)
        return mine, me_e + (lax.rem(mine + k, extent) - mine) * stride

    def head_start(stage):
        extent, stride = stages[stage]
        mine, _ = head_peer(stage, 0)
        head_recv[stage, mine] = head_part[...]
        for k in range(1, extent):
            pltpu.make_async_remote_copy(
                src_ref=head_part,
                dst_ref=head_recv.at[stage, mine],
                send_sem=head_send_sem.at[stage],
                recv_sem=head_recv_sem.at[stage],
                device_id={"expert": head_peer(stage, k)[1]},
                device_id_type=MESH,
            ).start()

    def head_finish(stage):
        extent, stride = stages[stage]
        block = head_recv.at[stage, pl.ds(0, extent - 1)]
        pltpu.make_async_copy(block, block, head_recv_sem.at[stage]).wait()
        pltpu.make_async_copy(block, block, head_send_sem.at[stage]).wait()
        total = head_recv[stage, 0]
        for k in range(1, extent):
            total = total + head_recv[stage, k]
        head_part[...] = total

    def chain_copy(way, layer, step):
        return pltpu.make_async_remote_copy(
            src_ref=chain_send.at[way, step, layer],
            dst_ref=chain_recv.at[way, step, layer],
            send_sem=chain_send_sem.at[way],
            recv_sem=chain_recv_sem.at[way, step, layer],
            device_id={"dp": below if way == 0 else above},
            device_id_type=MESH,
        )

    def shard_of(way, distance):
        if way == 0:
            return lax.rem(me_d + replicas - distance, replicas)
        return lax.rem(me_d + distance, replicas)

    def weight_grad(layer):
        upstream = acts[layers]
        part[layer] = matmul(acts[layer], upstream, ((0,), (0,))).reshape(replicas, piece, width)
        small[pl.ds(layer, 1), :] = upstream.astype(F32).sum(axis=0, keepdims=True)
        for way in range(2):
            if reach[way] > 0:
                chain_send[way, 0, layer] = part[layer, shard_of(way, reach[way])].astype(BF16)
                chain_copy(way, layer, 0).start()

    def backward(i, c):
        layer = layers - 1 - i
        weight_grad(layer)
        spread = matmul(acts[layers], w_ref[layer], ((1,), (1,)))
        acts[layers] = (spread * one_minus_exp(acts[layer].astype(F32))).astype(BF16)
        return c

    marks = [2, 4, layers - 1]
    head_start(0)
    done = 0
    for stage in range(3):
        lax.fori_loop(done, marks[stage], backward, 0)
        done = marks[stage]
        if stage < len(stages):
            head_finish(stage)
            if stage + 1 < len(stages):
                head_start(stage + 1)
    spread = matmul(acts[layers], w_ref[0], ((1,), (1,)))
    back_send[...] = spread.reshape(experts, cap, width).astype(BF16)
    exchange(3, back_send, back_recv)
    weight_grad(0)

    small[layers : layers + 8, :] = head_part[...]
    small_recv[me_d] = small[...]

    def small_start(k, c):
        peer = lax.rem(me_d + k, replicas)
        pltpu.make_async_remote_copy(
            src_ref=small,
            dst_ref=small_recv.at[me_d],
            send_sem=small_send_sem.at[0],
            recv_sem=small_recv_sem.at[0],
            device_id={"dp": peer},
            device_id_type=MESH,
        ).start()
        return c

    lax.fori_loop(1, replicas, small_start, 0)

    for step in range(1, max(reach)):

        def hop(i, c):
            layer = layers - 1 - i
            for way in range(2):
                if step < reach[way]:
                    chain_copy(way, layer, step - 1).wait_recv()
                    chain_send[way, step, layer] = (
                        chain_recv[way, step - 1, layer].astype(F32)
                        + part[layer, shard_of(way, reach[way] - step)]
                    ).astype(BF16)
                    chain_copy(way, layer, step).start()
            return c

        lax.fori_loop(0, layers, hop, 0)

    far = (reach[1], reach[0])

    def ring_copy(way, layer, step):
        owner = shard_of(1 - way, step)
        return pltpu.make_async_remote_copy(
            src_ref=out_w.at[owner, layer],
            dst_ref=out_w.at[owner, layer],
            send_sem=ring_send_sem.at[way],
            recv_sem=ring_recv_sem.at[way, step, layer],
            device_id={"dp": below if way == 0 else above},
            device_id_type=MESH,
        )

    def finish(i, c):
        layer = layers - 1 - i
        total = part[layer, me_d]
        for way in range(2):
            if reach[way] > 0:
                chain_copy(way, layer, reach[way] - 1).wait_recv()
                total = total + chain_recv[way, reach[way] - 1, layer].astype(F32)
        out_w[me_d, layer] = total.astype(BF16)
        for way in range(2):
            if far[way] > 0:
                ring_copy(way, layer, 0).start()
        return c

    lax.fori_loop(0, layers, finish, 0)
    for step in range(1, max(far)):

        def forward_on(i, c):
            layer = layers - 1 - i
            for way in range(2):
                if step < far[way]:
                    ring_arrive(way, layer, step - 1)
                    ring_copy(way, layer, step).start()
            return c

        def ring_arrive(way, layer, step):
            owner = shard_of(1 - way, step + 1)
            pltpu.make_async_copy(
                out_w.at[owner, layer], out_w.at[owner, layer], ring_recv_sem.at[way, step, layer]
            ).wait()

        lax.fori_loop(0, layers, forward_on, 0)

    arrive(3, back_send, back_recv)
    slots = back_recv[...].astype(F32).reshape(cells, width).astype(BF16)
    again = (lax.broadcasted_iota(jnp.int32, (cells, samples), 0) == cell).astype(BF16)
    out_in[...] = matmul(again, slots, ((0,), (0,))).astype(BF16)

    block = small_recv.at[pl.ds(0, replicas - 1)]
    pltpu.make_async_copy(block, block, small_recv_sem.at[0]).wait()
    total = small_recv[0]
    for k in range(1, replicas):
        total = total + small_recv[k]
    out_small[...] = total

    def last(i, c):
        layer = layers - 1 - i
        for way in range(2):
            if far[way] > 0:
                owner = shard_of(1 - way, far[way])
                pltpu.make_async_copy(
                    out_w.at[owner, layer],
                    out_w.at[owner, layer],
                    ring_recv_sem.at[way, far[way] - 1, layer],
                ).wait()
        return c

    lax.fori_loop(0, layers, last, 0)

    sent(0, row_send, row_recv)
    sent(1, up_send, up_recv)
    sent(2, down_send, down_recv)
    sent(3, back_send, back_recv)
    pltpu.make_async_copy(block, block, small_send_sem.at[0]).wait()
    for way in range(2):
        if reach[way] > 0:
            gone = chain_send.at[way, pl.ds(0, reach[way])]
            pltpu.make_async_copy(gone, gone, chain_send_sem.at[way]).wait()
        if far[way] > 0:
            gone = out_w.at[pl.ds(0, far[way])]
            pltpu.make_async_copy(gone, gone, ring_send_sem.at[way]).wait()


def per_device(
    replicas,
    experts,
    inputs,
    layer_weights,
    layer_biases,
    head_weight,
    head_bias,
    gate_values,
    spacing,
    ray_index,
    expert_index,
    slot_index,
    color_cotangent,
):
    samples, width = inputs.shape[2:]
    layers = layer_weights.shape[1]
    cap = 2 * samples // experts
    cells = experts * cap
    piece = width // replicas
    steps = replicas // 2
    lanes = 128
    dma = pltpu.SemaphoreType.DMA
    whole = pl.BlockSpec(memory_space=pltpu.VMEM)
    out_in, out_w, out_small = pl.pallas_call(
        functools.partial(body, replicas, experts),
        out_shape=(
            jax.ShapeDtypeStruct((samples, width), BF16),
            jax.ShapeDtypeStruct((replicas, layers, piece, width), BF16),
            jax.ShapeDtypeStruct((layers + 8, width), F32),
        ),
        in_specs=[whole] * 11,
        out_specs=(whole,) * 3,
        scratch_shapes=[
            pltpu.VMEM((layers + 1, cells, width), BF16),
            pltpu.VMEM((lanes, width), F32),
            pltpu.VMEM((experts, cap, width), BF16),
            pltpu.VMEM((experts, cap, width), BF16),
            pltpu.VMEM((experts, 1, lanes), F32),
            pltpu.VMEM((experts, 1, lanes), F32),
            pltpu.VMEM((experts, 1, lanes), F32),
            pltpu.VMEM((experts, 1, lanes), F32),
            pltpu.VMEM((experts, cap, width), BF16),
            pltpu.VMEM((experts, cap, width), BF16),
            pltpu.VMEM((layers, replicas, piece, width), F32),
            pltpu.VMEM((2, steps, layers, piece, width), BF16),
            pltpu.VMEM((2, steps, layers, piece, width), BF16),
            pltpu.VMEM((8, width), F32),
            pltpu.VMEM((3, 8, 8, width), F32),
            pltpu.VMEM((layers + 8, width), F32),
            pltpu.VMEM((replicas, layers + 8, width), F32),
            dma((4,)),
            dma((4,)),
            dma((2,)),
            dma((2, steps, layers)),
            dma((2,)),
            dma((2, steps, layers)),
            dma((3,)),
            dma((3,)),
            dma((1,)),
            dma((1,)),
        ],
        compiler_params=pltpu.CompilerParams(
            collective_id=0, has_side_effects=True, vmem_limit_bytes=56 * 1024 * 1024
        ),
    )(
        inputs.reshape(samples, width),
        layer_weights[0],
        layer_biases[0],
        head_weight,
        head_bias.reshape(1, 4),
        gate_values.reshape(1, samples),
        spacing.reshape(1, samples),
        ray_index.reshape(1, samples),
        expert_index.reshape(1, samples),
        slot_index.reshape(1, samples),
        color_cotangent.reshape(color_cotangent.shape[2:]),
    )
    grad_weights = out_w.transpose(1, 0, 2, 3).reshape(1, layers, width, width).astype(F32)
    return (
        out_in.reshape(1, 1, samples, width),
        grad_weights,
        out_small[None, :layers],
        out_small[layers : layers + 4],
        out_small[layers + 4 :, 0],
    )


def solution(mesh):
    in_specs = (
        P("dp", "expert", None, None),
        P("expert", None, None, None),
        P("expert", None, None),
        P(),
        P(),
        P("dp", "expert", None),
        P("dp", "expert", None),
        P("dp", "expert", None),
        P("dp", "expert", None),
        P("dp", "expert", None),
        P("dp", "expert", None, None),
    )
    out_specs = (
        P("dp", "expert", None, None),
        P("expert", None, None, None),
        P("expert", None, None),
        P(),
        P(),
    )
    return jax.shard_map(
        functools.partial(per_device, mesh.shape["dp"], mesh.shape["expert"]),
        mesh=mesh,
        in_specs=in_specs,
        out_specs=out_specs,
        check_vma=False,
    )
```

time: 232 us -> 95.1 us (0.41)
  blocking collectives: 140 us -> 0 us
  Pallas kernels: 0 us -> 85.4 us
  waiting for transfers between devices: 23.3 us -> 0 us
  starting transfers between devices: 22 us -> 0 us
  matrix products: 17.8 us -> 0 us
  between operations: 14.5 us -> 0.66 us
  local copies, waits for them, and re-layouts: 12.2 us -> 7.27 us
    psum x2 -> x0, blocking collectives: 123 us -> none  [the longest x1 106 us: per_device(): lax.psum((head_part, bias_part), ('dp', 'expert'))]
    pallas_call x0 -> x1, Pallas kernels: none -> 85.4 us  [per_device(): pl.pallas_call(functools.partial(body, replicas, experts), out_shape=(jax...]
    all_to_all x3 -> x0, waiting for transfers between devices: 23.3 us -> none  [the longest x1 12.1 us: per_device(): lax.all_to_all(features.reshape(experts, capacity, width), 'expert', spli...]
    all_to_all x3 -> x0, starting transfers between devices: 21.9 us -> none  [the longest x1 10.7 us: per_device(): lax.all_to_all(send_rows.reshape(experts, capacity, width), 'expert', spl...]
    dot_general x30 -> x0, matrix products: 17.8 us -> none  [the longest x8 6.99 us: forward(): jnp.dot(current, weights[number], preferred_element_type=jnp.float32)]
    all_to_all x1 -> x0, blocking collectives: 17.8 us -> none  [per_device(): lax.all_to_all(send_grads.reshape(experts, capacity, width), 'expert', sp...]
    scatter x2 -> x0, local copies, waits for them, and re-layouts: 3.69 us -> none  [the longest x1 2.14 us: per_device(): jnp.zeros((slot_total, width), jnp.bfloat16).at[cell_index].set(rows_local)]
    gather x2 -> x0, local copies, waits for them, and re-layouts: 2.96 us -> none  [the longest x1 1.81 us: per_device(): returned_grads.reshape(slot_total, width)[cell_index]]
  transfers between devices with their start and end apart: 4 -> 0, of which waited for: 2 -> 0; matrix products, arithmetic and copies ran while one was open for 2% -> 0% of each run, Pallas kernels for 0% -> 0%
where the time goes in v1:
time: 95.1 us; the launch traced here: 94.8 us
  Pallas kernels  85.4 us (90%)
  local copies, waits for them, and re-layouts  7.27 us (8%)
  other arithmetic  1.49 us (2%)
    pallas_call x1, Pallas kernels, per_device(): pl.pallas_call(functools.partial(body, replicas, experts), out_shape=(jax...  85.4 us
    unnamed x4, local copies, waits for them, and re-layouts  1.92 us

profile of v1, /device:TPU:2, one launch (start us, length us, event | category | flops | bytes accessed | tf_op | source)
XLA Modules:
  0.0 94.8 jit_solution(2475782983761450546)
XLA Ops:
  0.6 1.3 %copy.19 = f32[1,1,3,4]{3,2,1,0:T(4,128)} copy(f32[1,1,3,4]{3,1,2,0:T(1,128)} %param.21) | data formatting | bytes 96
  1.9 85.4 %shard_map.146 = (bf16[256,256]{1,0:T(8,128)(2,1)}, bf16[8,8,32,256]{3,2,1,0:T(8,128)(2,1)}, f32[16,256]{1,0:T(8,128)}) custom-call(bf16[256,256]{1,0:T(8,128)(2,1)} %bitcast.20, bf16[8,256,256]{2,1,0:T(8,128)(2,1)} %bitcast.19, f32[8,256]{1,0:T(8,128)} %bitcast.22, bf16[4,256]{1,0:T(4,128)(2,1)} %hw_ref.1, f32[1,4]{1,0:T(1,128)} %bitcast.29, ...), custom_call_target="tpu_custom_call" | custom-call | tf_op jit(solution)/shard_map/pallas_call | solution.py:471
  87.3 1.3 %slice_reduce_fusion = f32[4]{0:T(128)} fusion(f32[16,256]{1,0:T(8,128)} %get-tuple-element.10), kind=kLoop, calls=%fused_computation.3 | loop fusion | bytes 32 | tf_op jit(solution)/shard_map/slice | solution.py:531
  88.6 1.3 %slice.10 = f32[4,256]{1,0:T(4,128)} slice(f32[16,256]{1,0:T(8,128)} %get-tuple-element.10), slice={[8:12], [0:256]} | slice | bytes 8192 | tf_op jit(solution)/shard_map/slice | solution.py:530
  89.9 1.3 %slice_bitcast_fusion = f32[1,8,256]{2,1,0:T(8,128)} fusion(f32[16,256]{1,0:T(8,128)} %get-tuple-element.10), kind=kLoop, calls=%fused_computation.1 | loop fusion | bytes 16384 | tf_op jit(solution)/shard_map/broadcast_in_dim | solution.py:529
  91.2 1.5 %convert_bitcast_fusion = f32[8,8,32,256]{3,2,0,1:T(8,128)S(1)} fusion(bf16[8,8,32,256]{3,2,1,0:T(8,128)(2,1)} %get-tuple-element.9), kind=kLoop, calls=%fused_computation | loop fusion | flops 524288 | bytes 3145728 | tf_op jit(solution)/shard_map/convert_element_type | solution.py:525
  92.7 0.0 copy-start
  92.7 1.5 %copy.16 = f32[8,8,32,256]{3,2,1,0:T(8,128)} copy(f32[8,8,32,256]{3,2,0,1:T(8,128)S(1)} %convert_bitcast_fusion) | data formatting | bytes 4194304 | tf_op jit(solution)/shard_map/convert_element_type | solution.py:525
  94.2 0.0 copy-done
  94.2 0.7 copy.21
Async XLA Ops:
  92.7 1.5 %copy-start = (bf16[256,256]{1,0:T(8,128)(2,1)S(1)}, bf16[256,256]{1,0:T(8,128)(2,1)}, u32[]{:S(2)}) copy-start(bf16[256,256]{1,0:T(8,128)(2,1)} %get-tuple-element.8) | copy-start | bytes 393220

commit v2 on v1

--- a/solution.py
+++ b/solution.py
@@ -45,7 +45,7 @@
 
 
 def composite(unscaled, gate, hb_ref, spacing, ray, ct_ref):
-    rays = ct_ref.shape[1]
+    rays = ct_ref.shape[2]
     samples = ray.shape[1]
     logits = [gate * unscaled[h : h + 1, :] + hb_ref[0:1, h : h + 1] for h in range(4)]
     sigma = softplus(logits[0])
@@ -65,7 +65,7 @@
     for k in range(3):
         cotangent = jnp.zeros_like(weight)
         for r in range(rays):
-            cotangent += ct_ref[k : k + 1, r : r + 1] * hot[r : r + 1, :]
+            cotangent += ct_ref[k, 0:1, r : r + 1] * hot[r : r + 1, :]
         weight_grad += cotangent * colors[k]
         grads.append(cotangent * weight * colors[k] * (1.0 - colors[k]))
     inside_grad = -weight_grad * weight
@@ -80,6 +80,21 @@
 def body(
     replicas,
     experts,
+    *refs,
+):
+    sources, refs = refs[:11], refs[11:]
+    (out_in, out_w, out_small), refs = refs[:3], refs[3:]
+    loaded, (load_sem, *refs) = refs[:11], refs[11:]
+    loads = [pltpu.make_async_copy(a, b, load_sem.at[n]) for n, (a, b) in enumerate(zip(sources, loaded))]
+    for load in loads:
+        load.start()
+    compute(replicas, experts, loads, *loaded, out_in, out_w, out_small, *refs)
+
+
+def compute(
+    replicas,
+    experts,
+    loads,
     in_ref,
     w_ref,
     b_ref,
@@ -132,7 +147,11 @@
     me_e = lax.axis_index("expert")
     above = lax.rem(me_d + 1, replicas)
     below = lax.rem(me_d + replicas - 1, replicas)
-    reach = (replicas // 2, replicas - 1 - replicas // 2)
+    most = replicas // 2
+
+    def reach(way, layer):
+        return most - (layer + way) % 2
+
     stages = factors(experts)
 
     barrier = pltpu.get_barrier_semaphore()
@@ -169,13 +188,15 @@
         target[me_e] = source[me_e]
 
     def arrive(phase, source, target):
-        most = pl.ds(0, experts - 1)
-        pltpu.make_async_copy(source.at[most], target.at[most], a2a_recv_sem.at[phase]).wait()
+        peers = pl.ds(0, experts - 1)
+        pltpu.make_async_copy(source.at[peers], target.at[peers], a2a_recv_sem.at[phase]).wait()
 
     def sent(phase, source, target):
-        most = pl.ds(0, experts - 1)
-        pltpu.make_async_copy(source.at[most], target.at[most], a2a_send_sem.at[phase]).wait()
-
+        peers = pl.ds(0, experts - 1)
+        pltpu.make_async_copy(source.at[peers], target.at[peers], a2a_send_sem.at[phase]).wait()
+
+    for n in (0, 3, 8, 9):
+        loads[n].wait()
     cell = expert_ref[...] * cap + slot_ref[...]
     pick = (lax.broadcasted_iota(jnp.int32, (cells, samples), 0) == cell).astype(BF16)
     rows = matmul(pick, in_ref[...], ((1,), (0,)))
@@ -190,6 +211,9 @@
     arrive(0, row_send, row_recv)
     acts[0] = row_recv[...].astype(F32).reshape(cells, width).astype(BF16)
 
+    for n in (1, 2, 4, 5, 6, 7, 10):
+        loads[n].wait()
+
     def forward(layer, c):
         v = matmul(acts[layer], w_ref[layer], ((1,), (0,))) + b_ref[pl.ds(layer, 1), :]
         acts[layer + 1] = softplus(v).astype(BF16)
@@ -282,7 +306,7 @@
 
     def chain_copy(way, layer, step):
         return pltpu.make_async_remote_copy(
-            src_ref=chain_send.at[way, step, layer],
+            src_ref=chain_send.at[way, step * layers + layer],
             dst_ref=chain_recv.at[way, step, layer],
             send_sem=chain_send_sem.at[way],
             recv_sem=chain_recv_sem.at[way, step, layer],
@@ -300,9 +324,8 @@
         part[layer] = matmul(acts[layer], upstream, ((0,), (0,))).reshape(replicas, piece, width)
         small[pl.ds(layer, 1), :] = upstream.astype(F32).sum(axis=0, keepdims=True)
         for way in range(2):
-            if reach[way] > 0:
-                chain_send[way, 0, layer] = part[layer, shard_of(way, reach[way])].astype(BF16)
-                chain_copy(way, layer, 0).start()
+            chain_send[way, layer] = part[layer, shard_of(way, reach(way, layer))].astype(BF16)
+            chain_copy(way, layer, 0).start()
 
     def backward(i, c):
         layer = layers - 1 - i
@@ -343,23 +366,27 @@
 
     lax.fori_loop(1, replicas, small_start, 0)
 
-    for step in range(1, max(reach)):
-
-        def hop(i, c):
-            layer = layers - 1 - i
+    def by_pairs(step_of):
+        def pair(i, c):
+            for odd in (1, 0):
+                step_of(layers - 2 - 2 * i + odd, odd)
+            return c
+
+        lax.fori_loop(0, layers // 2, pair, 0)
+
+    for step in range(1, most):
+
+        def hop(layer, odd):
             for way in range(2):
-                if step < reach[way]:
+                if step < reach(way, odd):
                     chain_copy(way, layer, step - 1).wait_recv()
-                    chain_send[way, step, layer] = (
+                    chain_send[way, step * layers + layer] = (
                         chain_recv[way, step - 1, layer].astype(F32)
-                        + part[layer, shard_of(way, reach[way] - step)]
+                        + part[layer, shard_of(way, reach(way, odd) - step)]
                     ).astype(BF16)
                     chain_copy(way, layer, step).start()
-            return c
-
-        lax.fori_loop(0, layers, hop, 0)
-
-    far = (reach[1], reach[0])
+
+        by_pairs(hop)
 
     def ring_copy(way, layer, step):
         owner = shard_of(1 - way, step)
@@ -372,37 +399,31 @@
             device_id_type=MESH,
         )
 
-    def finish(i, c):
-        layer = layers - 1 - i
+    def ring_arrive(way, layer, step):
+        owner = shard_of(1 - way, step + 1)
+        pltpu.make_async_copy(
+            out_w.at[owner, layer], out_w.at[owner, layer], ring_recv_sem.at[way, step, layer]
+        ).wait()
+
+    def finish(layer, odd):
         total = part[layer, me_d]
         for way in range(2):
-            if reach[way] > 0:
-                chain_copy(way, layer, reach[way] - 1).wait_recv()
-                total = total + chain_recv[way, reach[way] - 1, layer].astype(F32)
+            chain_copy(way, layer, reach(way, odd) - 1).wait_recv()
+            total = total + chain_recv[way, reach(way, odd) - 1, layer].astype(F32)
         out_w[me_d, layer] = total.astype(BF16)
         for way in range(2):
-            if far[way] > 0:
-                ring_copy(way, layer, 0).start()
-        return c
-
-    lax.fori_loop(0, layers, finish, 0)
-    for step in range(1, max(far)):
-
-        def forward_on(i, c):
-            layer = layers - 1 - i
+            ring_copy(way, layer, 0).start()
+
+    by_pairs(finish)
+    for step in range(1, most):
+
+        def forward_on(layer, odd):
             for way in range(2):
-                if step < far[way]:
+                if step < reach(way, odd):
                     ring_arrive(way, layer, step - 1)
                     ring_copy(way, layer, step).start()
-            return c
-
-        def ring_arrive(way, layer, step):
-            owner = shard_of(1 - way, step + 1)
-            pltpu.make_async_copy(
-                out_w.at[owner, layer], out_w.at[owner, layer], ring_recv_sem.at[way, step, layer]
-            ).wait()
-
-        lax.fori_loop(0, layers, forward_on, 0)
+
+        by_pairs(forward_on)
 
     arrive(3, back_send, back_recv)
     slots = back_recv[...].astype(F32).reshape(cells, width).astype(BF16)
@@ -416,19 +437,11 @@
         total = total + small_recv[k]
     out_small[...] = total
 
-    def last(i, c):
-        layer = layers - 1 - i
+    def last(layer, odd):
         for way in range(2):
-            if far[way] > 0:
-                owner = shard_of(1 - way, far[way])
-                pltpu.make_async_copy(
-                    out_w.at[owner, layer],
-                    out_w.at[owner, layer],
-                    ring_recv_sem.at[way, far[way] - 1, layer],
-                ).wait()
-        return c
-
-    lax.fori_loop(0, layers, last, 0)
+            ring_arrive(way, layer, reach(way, odd) - 1)
+
+    by_pairs(last)
 
     sent(0, row_send, row_recv)
     sent(1, up_send, up_recv)
@@ -436,12 +449,28 @@
     sent(3, back_send, back_recv)
     pltpu.make_async_copy(block, block, small_send_sem.at[0]).wait()
     for way in range(2):
-        if reach[way] > 0:
-            gone = chain_send.at[way, pl.ds(0, reach[way])]
-            pltpu.make_async_copy(gone, gone, chain_send_sem.at[way]).wait()
-        if far[way] > 0:
-            gone = out_w.at[pl.ds(0, far[way])]
-            pltpu.make_async_copy(gone, gone, ring_send_sem.at[way]).wait()
+        gone = chain_send.at[way, pl.ds(0, most * layers - layers // 2)]
+        pltpu.make_async_copy(gone, gone, chain_send_sem.at[way]).wait()
+        pltpu.make_async_copy(gone, gone, ring_send_sem.at[way]).wait()
+
+
+def write_out(
+    in_ref, w_ref, small_ref, out_in, out_w, out_b, out_hw, out_hb, wide, out_sem
+):
+    layers = wide.shape[0]
+    stores = [
+        pltpu.make_async_copy(wide.at[n], out_w.at[n], out_sem.at[n]) for n in range(layers)
+    ]
+    for n in range(layers):
+        wide[n] = w_ref[:, n].astype(F32)
+        stores[n].start()
+    out_in[...] = in_ref[...]
+    out_b[...] = small_ref[0:layers, :]
+    out_hw[...] = small_ref[layers : layers + 4, :]
+    for h in range(4):
+        out_hb[0:1, h : h + 1] = small_ref[layers + 4 + h : layers + 5 + h, 0:1]
+    for store in stores:
+        store.wait()
 
 
 def per_device(
@@ -467,6 +496,19 @@
     steps = replicas // 2
     lanes = 128
     dma = pltpu.SemaphoreType.DMA
+    operands = (
+        inputs.reshape(samples, width),
+        layer_weights[0],
+        layer_biases[0],
+        head_weight,
+        head_bias.reshape(1, 4),
+        gate_values.reshape(1, samples),
+        spacing.reshape(1, samples),
+        ray_index.reshape(1, samples),
+        expert_index.reshape(1, samples),
+        slot_index.reshape(1, samples),
+        color_cotangent.reshape(3, 1, color_cotangent.shape[3]),
+    )
     whole = pl.BlockSpec(memory_space=pltpu.VMEM)
     out_in, out_w, out_small = pl.pallas_call(
         functools.partial(body, replicas, experts),
@@ -475,9 +517,11 @@
             jax.ShapeDtypeStruct((replicas, layers, piece, width), BF16),
             jax.ShapeDtypeStruct((layers + 8, width), F32),
         ),
-        in_specs=[whole] * 11,
+        in_specs=[pl.BlockSpec(memory_space=pltpu.HBM)] * 11,
         out_specs=(whole,) * 3,
         scratch_shapes=[
+            *(pltpu.VMEM(a.shape, a.dtype) for a in operands),
+            dma((11,)),
             pltpu.VMEM((layers + 1, cells, width), BF16),
             pltpu.VMEM((lanes, width), F32),
             pltpu.VMEM((experts, cap, width), BF16),
@@ -489,7 +533,7 @@
             pltpu.VMEM((experts, cap, width), BF16),
             pltpu.VMEM((experts, cap, width), BF16),
             pltpu.VMEM((layers, replicas, piece, width), F32),
-            pltpu.VMEM((2, steps, layers, piece, width), BF16),
+            pltpu.VMEM((2, steps * layers, piece, width), BF16),
             pltpu.VMEM((2, steps, layers, piece, width), BF16),
             pltpu.VMEM((8, width), F32),
             pltpu.VMEM((3, 8, 8, width), F32),
@@ -507,28 +551,32 @@
             dma((1,)),
         ],
         compiler_params=pltpu.CompilerParams(
-            collective_id=0, has_side_effects=True, vmem_limit_bytes=56 * 1024 * 1024
+            collective_id=0, has_side_effects=True, vmem_limit_bytes=32 * 1024 * 1024
         ),
-    )(
-        inputs.reshape(samples, width),
-        layer_weights[0],
-        layer_biases[0],
-        head_weight,
-        head_bias.reshape(1, 4),
-        gate_values.reshape(1, samples),
-        spacing.reshape(1, samples),
-        ray_index.reshape(1, samples),
-        expert_index.reshape(1, samples),
-        slot_index.reshape(1, samples),
-        color_cotangent.reshape(color_cotangent.shape[2:]),
-    )
-    grad_weights = out_w.transpose(1, 0, 2, 3).reshape(1, layers, width, width).astype(F32)
+    )(*(pltpu.with_memory_space_constraint(a, pltpu.HBM) for a in operands))
+    grad_inputs, grad_weights, grad_biases, grad_head_weight, grad_head_bias = pl.pallas_call(
+        write_out,
+        out_shape=(
+            jax.ShapeDtypeStruct((samples, width), BF16),
+            jax.ShapeDtypeStruct((layers, replicas, piece, width), F32),
+            jax.ShapeDtypeStruct((layers, width), F32),
+            jax.ShapeDtypeStruct((4, width), F32),
+            jax.ShapeDtypeStruct((1, 4), F32),
+        ),
+        in_specs=[whole] * 3,
+        out_specs=(whole, pl.BlockSpec(memory_space=pl.ANY), whole, whole, whole),
+        scratch_shapes=[
+            pltpu.VMEM((layers, replicas, piece, width), F32),
+            dma((layers,)),
+        ],
+        compiler_params=pltpu.CompilerParams(vmem_limit_bytes=16 * 1024 * 1024),
+    )(out_in, out_w, out_small)
     return (
-        out_in.reshape(1, 1, samples, width),
-        grad_weights,
-        out_small[None, :layers],
-        out_small[layers : layers + 4],
-        out_small[layers + 4 :, 0],
+        grad_inputs.reshape(1, 1, samples, width),
+        grad_weights.reshape(1, layers, width, width),
+        grad_biases[None],
+        grad_head_weight,
+        grad_head_bias.reshape(4),
     )
 
 

time: 95.1 us -> 87.2 us (0.917)
  local copies, waits for them, and re-layouts: 7.27 us -> 0 us
  other arithmetic: 1.49 us -> 0 us
  Pallas kernels: 85.4 us -> 86.4 us
    slice x2 -> x0, local copies, waits for them, and re-layouts: 2.6 us -> none  [the longest x1 1.31 us: per_device(): out_small[layers + 4:, 0]]
    pallas_call x0 -> x1, Pallas kernels: none -> 2.06 us  [per_device(): pl.pallas_call(write_out, out_shape=(jax.ShapeDtypeStruct((samples, width...]
    unnamed x4 -> x0, local copies, waits for them, and re-layouts: 1.92 us -> none
    convert_element_type x1 -> x0, other arithmetic: 1.49 us -> none  [per_device(): out_w.transpose(1, 0, 2, 3).reshape(1, layers, width, width).astype(F32)]
    convert_element_type x1 -> x0, local copies, waits for them, and re-layouts: 1.46 us -> none  [per_device(): out_w.transpose(1, 0, 2, 3).reshape(1, layers, width, width).astype(F32)]
    broadcast_in_dim x1 -> x0, local copies, waits for them, and re-layouts: 1.29 us -> none  [per_device(): out_small[None, :layers]]
    pallas_call x1, Pallas kernels: 85.4 us -> 84.4 us  [per_device(): pl.pallas_call(functools.partial(body, replicas, experts), out_shape=(jax...]
where the time goes in v2:
time: 87.2 us; the launch traced here: 87.1 us
  Pallas kernels  86.4 us (99%)
    pallas_call x1, Pallas kernels, per_device(): pl.pallas_call(functools.partial(body, replicas, experts), out_shape=(jax...  84.4 us
    pallas_call x1, Pallas kernels, per_device(): pl.pallas_call(write_out, out_shape=(jax.ShapeDtypeStruct((samples, width...  2.06 us

profile of v2, /device:TPU:2, one launch (start us, length us, event | category | flops | bytes accessed | tf_op | source)
XLA Modules:
  0.0 87.1 jit_solution(7645817497538281636)
XLA Ops:
  0.6 84.4 %shard_map.146 = (bf16[256,256]{1,0:T(8,128)(2,1)S(1)}, bf16[8,8,32,256]{3,2,1,0:T(8,128)(2,1)S(1)}, f32[16,256]{1,0:T(8,128)S(1)}) custom-call(bf16[256,256]{1,0:T(8,128)(2,1)} %bitcast.15, bf16[8,256,256]{2,1,0:T(8,128)(2,1)} %bitcast.14, f32[8,256]{1,0:T(8,128)} %bitcast.16, bf16[4,256]{1,0:T(4,128)(2,1)} %refs_3_.1, f32[1,4]{1,0:T(1,128)} %bitcast.23, ...), custom_call_target="tpu_custom_call" | custom-call | tf_op jit(solution)/shard_map/pallas_call | solution.py:513
  85.0 2.1 %shard_map.147 = (bf16[256,256]{1,0:T(8,128)(2,1)}, f32[8,8,32,256]{3,2,1,0:T(8,128)}, f32[8,256]{1,0:T(8,128)}, f32[4,256]{1,0:T(4,128)}, f32[1,4]{1,0:T(1,128)}) custom-call(bf16[256,256]{1,0:T(8,128)(2,1)S(1)} %get-tuple-element.13.in_ref, bf16[8,8,32,256]{3,2,1,0:T(8,128)(2,1)S(1)} %get-tuple-element.14.w_ref, f32[16,256]{1,0:T(8,128)S(1)} %get-tuple-element.15.small_ref), custom_call_target="tpu_custom_call" | custom-call | tf_op jit(solution)/shard_map/pallas_call | solution.py:557

commit v3 on v2

--- a/solution.py
+++ b/solution.py
@@ -173,19 +173,23 @@
 
     def exchange(phase, source, target):
         def send(k, c):
-            peer = lax.rem(me_e + k, experts)
-            pltpu.make_async_remote_copy(
-                src_ref=source.at[peer],
-                dst_ref=target.at[me_e],
-                send_sem=a2a_send_sem.at[phase],
-                recv_sem=a2a_recv_sem.at[phase],
-                device_id={"expert": peer},
-                device_id_type=MESH,
-            ).start()
+            exchange_one(phase, source, target, k)
             return c
 
         lax.fori_loop(1, experts, send, 0)
         target[me_e] = source[me_e]
+
+    def exchange_one(phase, source, target, k):
+        ahead = experts // 2 - k // 2
+        peer = lax.rem(me_e + experts + ahead * (1 - 2 * (k % 2)), experts)
+        pltpu.make_async_remote_copy(
+            src_ref=source.at[peer],
+            dst_ref=target.at[me_e],
+            send_sem=a2a_send_sem.at[phase],
+            recv_sem=a2a_recv_sem.at[phase],
+            device_id={"expert": peer},
+            device_id_type=MESH,
+        ).start()
 
     def arrive(phase, source, target):
         peers = pl.ds(0, experts - 1)
@@ -322,23 +326,45 @@
     def weight_grad(layer):
         upstream = acts[layers]
         part[layer] = matmul(acts[layer], upstream, ((0,), (0,))).reshape(replicas, piece, width)
-        small[pl.ds(layer, 1), :] = upstream.astype(F32).sum(axis=0, keepdims=True)
+        small[lax.rem(layer, replicas), pl.ds(layer // replicas, 1), :] = upstream.astype(F32).sum(
+            axis=0, keepdims=True
+        )
         for way in range(2):
             chain_send[way, layer] = part[layer, shard_of(way, reach(way, layer))].astype(BF16)
             chain_copy(way, layer, 0).start()
 
-    def backward(i, c):
-        layer = layers - 1 - i
-        weight_grad(layer)
-        spread = matmul(acts[layers], w_ref[layer], ((1,), (1,)))
-        acts[layers] = (spread * one_minus_exp(acts[layer].astype(F32))).astype(BF16)
-        return c
-
-    marks = [2, 4, layers - 1]
+    def hop(step, layer, way):
+        chain_copy(way, layer, step - 1).wait_recv()
+        chain_send[way, step * layers + layer] = (
+            chain_recv[way, step - 1, layer].astype(F32)
+            + part[layer, shard_of(way, reach(way, layer) - step)]
+        ).astype(BF16)
+        chain_copy(way, layer, step).start()
+
+    lag = 3
+
+    def hops(i, count):
+        for step in range(1, most - 1):
+            if step <= count:
+                for way in range(2):
+                    hop(step, layers - 1 - (i - lag * step), way)
+
+    def backward_with(count):
+        def backward(i, c):
+            layer = layers - 1 - i
+            weight_grad(layer)
+            hops(i, count)
+            spread = matmul(acts[layers], w_ref[layer], ((1,), (1,)))
+            acts[layers] = (spread * one_minus_exp(acts[layer].astype(F32))).astype(BF16)
+            return c
+
+        return backward
+
+    marks = [lag, 2 * lag, layers - 1]
     head_start(0)
     done = 0
     for stage in range(3):
-        lax.fori_loop(done, marks[stage], backward, 0)
+        lax.fori_loop(done, marks[stage], backward_with(stage), 0)
         done = marks[stage]
         if stage < len(stages):
             head_finish(stage)
@@ -346,16 +372,21 @@
                 head_start(stage + 1)
     spread = matmul(acts[layers], w_ref[0], ((1,), (1,)))
     back_send[...] = spread.reshape(experts, cap, width).astype(BF16)
-    exchange(3, back_send, back_recv)
+    back_recv[me_e] = back_send[me_e]
     weight_grad(0)
-
-    small[layers : layers + 8, :] = head_part[...]
-    small_recv[me_d] = small[...]
+    hops(layers - 1, 2)
+
+    for row in range(8):
+        place = layers + row
+        small[place % replicas, place // replicas : place // replicas + 1, :] = head_part[
+            row : row + 1, :
+        ]
+    small_recv[me_d] = small[me_d]
 
     def small_start(k, c):
         peer = lax.rem(me_d + k, replicas)
         pltpu.make_async_remote_copy(
-            src_ref=small,
+            src_ref=small.at[peer],
             dst_ref=small_recv.at[me_d],
             send_sem=small_send_sem.at[0],
             recv_sem=small_recv_sem.at[0],
@@ -366,27 +397,68 @@
 
     lax.fori_loop(1, replicas, small_start, 0)
 
-    def by_pairs(step_of):
+    work = sum(lag * step for step in range(1, most - 1)) + layers
+    per_slot = pl.cdiv(experts - 1, work)
+
+    def feed(slot):
+        for n in range(per_slot):
+            k = 1 + slot * per_slot + n
+
+            @pl.when(k < experts)
+            def _():
+                exchange_one(3, back_send, back_recv, k)
+
+    def by_pairs(step_of, first_slot=None):
         def pair(i, c):
             for odd in (1, 0):
                 step_of(layers - 2 - 2 * i + odd, odd)
+            if first_slot is not None:
+                feed(first_slot + i)
             return c
 
         lax.fori_loop(0, layers // 2, pair, 0)
 
-    for step in range(1, most):
-
-        def hop(layer, odd):
+    slot = 0
+    for step in range(1, most - 1):
+
+        def remaining(i, c):
             for way in range(2):
-                if step < reach(way, odd):
-                    chain_copy(way, layer, step - 1).wait_recv()
-                    chain_send[way, step * layers + layer] = (
-                        chain_recv[way, step - 1, layer].astype(F32)
-                        + part[layer, shard_of(way, reach(way, odd) - step)]
-                    ).astype(BF16)
-                    chain_copy(way, layer, step).start()
-
-        by_pairs(hop)
+                hop(step, layers - 1 - i, way)
+            feed(slot + i - (layers - lag * step))
+            return c
+
+        begin = layers - lag * step
+        lax.fori_loop(begin, layers, remaining, 0)
+        slot += layers - begin
+
+    def last_hop(layer, odd):
+        for way in range(2):
+            if most - 1 < reach(way, odd):
+                hop(most - 1, layer, way)
+
+    if most > 1:
+        by_pairs(last_hop, slot)
+        slot += layers // 2
+
+    peers_d = small_recv.at[pl.ds(0, replicas - 1)]
+    pltpu.make_async_copy(peers_d, peers_d, small_recv_sem.at[0]).wait()
+    total = small_recv[0]
+    for k in range(1, replicas):
+        total = total + small_recv[k]
+    out_small[me_d] = total
+
+    def small_spread(k, c):
+        pltpu.make_async_remote_copy(
+            src_ref=out_small.at[me_d],
+            dst_ref=out_small.at[me_d],
+            send_sem=small_send_sem.at[1],
+            recv_sem=small_recv_sem.at[1],
+            device_id={"dp": lax.rem(me_d + k, replicas)},
+            device_id_type=MESH,
+        ).start()
+        return c
+
+    lax.fori_loop(1, replicas, small_spread, 0)
 
     def ring_copy(way, layer, step):
         owner = shard_of(1 - way, step)
@@ -414,7 +486,7 @@
         for way in range(2):
             ring_copy(way, layer, 0).start()
 
-    by_pairs(finish)
+    by_pairs(finish, slot)
     for step in range(1, most):
 
         def forward_on(layer, odd):
@@ -430,12 +502,7 @@
     again = (lax.broadcasted_iota(jnp.int32, (cells, samples), 0) == cell).astype(BF16)
     out_in[...] = matmul(again, slots, ((0,), (0,))).astype(BF16)
 
-    block = small_recv.at[pl.ds(0, replicas - 1)]
-    pltpu.make_async_copy(block, block, small_recv_sem.at[0]).wait()
-    total = small_recv[0]
-    for k in range(1, replicas):
-        total = total + small_recv[k]
-    out_small[...] = total
+    pltpu.make_async_copy(peers_d, peers_d, small_recv_sem.at[1]).wait()
 
     def last(layer, odd):
         for way in range(2):
@@ -447,7 +514,8 @@
     sent(1, up_send, up_recv)
     sent(2, down_send, down_recv)
     sent(3, back_send, back_recv)
-    pltpu.make_async_copy(block, block, small_send_sem.at[0]).wait()
+    for n in range(2):
+        pltpu.make_async_copy(peers_d, peers_d, small_send_sem.at[n]).wait()
     for way in range(2):
         gone = chain_send.at[way, pl.ds(0, most * layers - layers // 2)]
         pltpu.make_async_copy(gone, gone, chain_send_sem.at[way]).wait()
@@ -465,10 +533,16 @@
         wide[n] = w_ref[:, n].astype(F32)
         stores[n].start()
     out_in[...] = in_ref[...]
-    out_b[...] = small_ref[0:layers, :]
-    out_hw[...] = small_ref[layers : layers + 4, :]
+    replicas = small_ref.shape[0]
+
+    def row(place):
+        return small_ref[place % replicas, place // replicas : place // replicas + 1, :]
+
+    for n in range(layers):
+        out_b[n : n + 1, :] = row(n)
     for h in range(4):
-        out_hb[0:1, h : h + 1] = small_ref[layers + 4 + h : layers + 5 + h, 0:1]
+        out_hw[h : h + 1, :] = row(layers + h)
+        out_hb[0:1, h : h + 1] = row(layers + 4 + h)[:, 0:1]
     for store in stores:
         store.wait()
 
@@ -515,7 +589,7 @@
         out_shape=(
             jax.ShapeDtypeStruct((samples, width), BF16),
             jax.ShapeDtypeStruct((replicas, layers, piece, width), BF16),
-            jax.ShapeDtypeStruct((layers + 8, width), F32),
+            jax.ShapeDtypeStruct((replicas, (layers + 8) // replicas, width), F32),
         ),
         in_specs=[pl.BlockSpec(memory_space=pltpu.HBM)] * 11,
         out_specs=(whole,) * 3,
@@ -537,8 +611,8 @@
             pltpu.VMEM((2, steps, layers, piece, width), BF16),
             pltpu.VMEM((8, width), F32),
             pltpu.VMEM((3, 8, 8, width), F32),
-            pltpu.VMEM((layers + 8, width), F32),
-            pltpu.VMEM((replicas, layers + 8, width), F32),
+            pltpu.VMEM((replicas, (layers + 8) // replicas, width), F32),
+            pltpu.VMEM((replicas, (layers + 8) // replicas, width), F32),
             dma((4,)),
             dma((4,)),
             dma((2,)),
@@ -547,8 +621,8 @@
             dma((2, steps, layers)),
             dma((3,)),
             dma((3,)),
-            dma((1,)),
-            dma((1,)),
+            dma((2,)),
+            dma((2,)),
         ],
         compiler_params=pltpu.CompilerParams(
             collective_id=0, has_side_effects=True, vmem_limit_bytes=32 * 1024 * 1024

time: 87.2 us -> 82.2 us (0.943)
  the two profiles are of different devices: /device:TPU:2 before, /device:TPU:8 now
where the time goes in v3:
time: 82.2 us; the launch traced here: 82.1 us
  Pallas kernels  81.4 us (99%)
    pallas_call x1, Pallas kernels, per_device(): pl.pallas_call(functools.partial(body, replicas, experts), out_shape=(jax...  79.4 us
    pallas_call x1, Pallas kernels, per_device(): pl.pallas_call(write_out, out_shape=(jax.ShapeDtypeStruct((samples, width...  2.06 us

profile of v3, /device:TPU:8, one launch (start us, length us, event | category | flops | bytes accessed | tf_op | source)
XLA Modules:
  0.0 82.1 jit_solution(4501765387119325693)
XLA Ops:
  0.6 79.4 %shard_map.146 = (bf16[256,256]{1,0:T(8,128)(2,1)S(1)}, bf16[8,8,32,256]{3,2,1,0:T(8,128)(2,1)S(1)}, f32[8,2,256]{2,1,0:T(2,128)S(1)}) custom-call(bf16[256,256]{1,0:T(8,128)(2,1)} %bitcast.15, bf16[8,256,256]{2,1,0:T(8,128)(2,1)} %bitcast.14, f32[8,256]{1,0:T(8,128)} %bitcast.16, bf16[4,256]{1,0:T(4,128)(2,1)} %refs_3_.1, f32[1,4]{1,0:T(1,128)} %bitcast.23, ...), custom_call_target="tpu_custom_call" | custom-call | tf_op jit(solution)/shard_map/pallas_call | solution.py:587
  80.0 2.1 %shard_map.147 = (bf16[256,256]{1,0:T(8,128)(2,1)}, f32[8,8,32,256]{3,2,1,0:T(8,128)}, f32[8,256]{1,0:T(8,128)}, f32[4,256]{1,0:T(4,128)}, f32[1,4]{1,0:T(1,128)}) custom-call(bf16[256,256]{1,0:T(8,128)(2,1)S(1)} %get-tuple-element.13.in_ref, bf16[8,8,32,256]{3,2,1,0:T(8,128)(2,1)S(1)} %get-tuple-element.14.w_ref, f32[8,2,256]{2,1,0:T(2,128)S(1)} %get-tuple-element.15.small_ref), custom_call_target="tpu_custom_call" | custom-call | tf_op jit(solution)/shard_map/pallas_call | solution.py:631

commit v4 on v3

--- a/solution.py
+++ b/solution.py
@@ -347,7 +347,7 @@
         for step in range(1, most - 1):
             if step <= count:
                 for way in range(2):
-                    hop(step, layers - 1 - (i - lag * step), way)
+                    pass
 
     def backward_with(count):
         def backward(i, c):
@@ -366,7 +366,7 @@
     for stage in range(3):
         lax.fori_loop(done, marks[stage], backward_with(stage), 0)
         done = marks[stage]
-        if stage < len(stages):
+        if stage < len(stages) and stage < 2:
             head_finish(stage)
             if stage + 1 < len(stages):
                 head_start(stage + 1)
@@ -376,6 +376,47 @@
     weight_grad(0)
     hops(layers - 1, 2)
 
+    work = sum(layers for step in range(1, most - 1)) + layers
+    per_slot = pl.cdiv(experts - 1, work)
+
+    def feed(slot):
+        for n in range(per_slot):
+            k = 1 + slot * per_slot + n
+
+            @pl.when(k < experts)
+            def _():
+                exchange_one(3, back_send, back_recv, k)
+
+    def by_pairs(step_of, first_slot=None):
+        def pair(i, c):
+            for odd in (1, 0):
+                step_of(layers - 2 - 2 * i + odd, odd)
+            if first_slot is not None:
+                feed(first_slot + i)
+            return c
+
+        lax.fori_loop(0, layers // 2, pair, 0)
+
+    slot = 0
+    for step in range(1, most - 1):
+
+        def remaining(i, c):
+            for way in range(2):
+                hop(step, layers - 1 - i, way)
+            feed(slot + i)
+            return c
+
+        begin = 0
+        lax.fori_loop(begin, layers, remaining, 0)
+        slot += layers - begin
+
+    def last_hop(layer, odd):
+        for way in range(2):
+            if most - 1 < reach(way, odd):
+                hop(most - 1, layer, way)
+
+    if len(stages) > 2:
+        head_finish(2)
     for row in range(8):
         place = layers + row
         small[place % replicas, place // replicas : place // replicas + 1, :] = head_part[
@@ -397,48 +438,37 @@
 
     lax.fori_loop(1, replicas, small_start, 0)
 
-    work = sum(lag * step for step in range(1, most - 1)) + layers
-    per_slot = pl.cdiv(experts - 1, work)
-
-    def feed(slot):
-        for n in range(per_slot):
-            k = 1 + slot * per_slot + n
-
-            @pl.when(k < experts)
-            def _():
-                exchange_one(3, back_send, back_recv, k)
-
-    def by_pairs(step_of, first_slot=None):
-        def pair(i, c):
-            for odd in (1, 0):
-                step_of(layers - 2 - 2 * i + odd, odd)
-            if first_slot is not None:
-                feed(first_slot + i)
-            return c
-
-        lax.fori_loop(0, layers // 2, pair, 0)
-
-    slot = 0
-    for step in range(1, most - 1):
-
-        def remaining(i, c):
-            for way in range(2):
-                hop(step, layers - 1 - i, way)
-            feed(slot + i - (layers - lag * step))
-            return c
-
-        begin = layers - lag * step
-        lax.fori_loop(begin, layers, remaining, 0)
-        slot += layers - begin
-
-    def last_hop(layer, odd):
-        for way in range(2):
-            if most - 1 < reach(way, odd):
-                hop(most - 1, layer, way)
-
     if most > 1:
         by_pairs(last_hop, slot)
         slot += layers // 2
+
+    def ring_copy(way, layer, step):
+        owner = shard_of(1 - way, step)
+        return pltpu.make_async_remote_copy(
+            src_ref=out_w.at[owner, layer],
+            dst_ref=out_w.at[owner, layer],
+            send_sem=ring_send_sem.at[way],
+            recv_sem=ring_recv_sem.at[way, step, layer],
+            device_id={"dp": below if way == 0 else above},
+            device_id_type=MESH,
+        )
+
+    def ring_arrive(way, layer, step):
+        owner = shard_of(1 - way, step + 1)
+        pltpu.make_async_copy(
+            out_w.at[owner, layer], out_w.at[owner, layer], ring_recv_sem.at[way, step, layer]
+        ).wait()
+
+    def finish(layer, odd):
+        total = part[layer, me_d]
+        for way in range(2):
+            chain_copy(way, layer, reach(way, odd) - 1).wait_recv()
+            total = total + chain_recv[way, reach(way, odd) - 1, layer].astype(F32)
+        out_w[me_d, layer] = total.astype(BF16)
+        for way in range(2):
+            ring_copy(way, layer, 0).start()
+
+    by_pairs(finish, slot)
 
     peers_d = small_recv.at[pl.ds(0, replicas - 1)]
     pltpu.make_async_copy(peers_d, peers_d, small_recv_sem.at[0]).wait()
@@ -460,33 +490,6 @@
 
     lax.fori_loop(1, replicas, small_spread, 0)
 
-    def ring_copy(way, layer, step):
-        owner = shard_of(1 - way, step)
-        return pltpu.make_async_remote_copy(
-            src_ref=out_w.at[owner, layer],
-            dst_ref=out_w.at[owner, layer],
-            send_sem=ring_send_sem.at[way],
-            recv_sem=ring_recv_sem.at[way, step, layer],
-            device_id={"dp": below if way == 0 else above},
-            device_id_type=MESH,
-        )
-
-    def ring_arrive(way, layer, step):
-        owner = shard_of(1 - way, step + 1)
-        pltpu.make_async_copy(
-            out_w.at[owner, layer], out_w.at[owner, layer], ring_recv_sem.at[way, step, layer]
-        ).wait()
-
-    def finish(layer, odd):
-        total = part[layer, me_d]
-        for way in range(2):
-            chain_copy(way, layer, reach(way, odd) - 1).wait_recv()
-            total = total + chain_recv[way, reach(way, odd) - 1, layer].astype(F32)
-        out_w[me_d, layer] = total.astype(BF16)
-        for way in range(2):
-            ring_copy(way, layer, 0).start()
-
-    by_pairs(finish, slot)
     for step in range(1, most):
 
         def forward_on(layer, odd):

time: 82.2 us -> 78.1 us (0.950)
  Pallas kernels: 81.4 us -> 77.3 us
    pallas_call x1, Pallas kernels: 79.4 us -> 75.3 us  [per_device(): pl.pallas_call(functools.partial(body, replicas, experts), out_shape=(jax...]
where the time goes in v4:
time: 78.1 us; the launch traced here: 78 us
  Pallas kernels  77.3 us (99%)
    pallas_call x1, Pallas kernels, per_device(): pl.pallas_call(functools.partial(body, replicas, experts), out_shape=(jax...  75.3 us
    pallas_call x1, Pallas kernels, per_device(): pl.pallas_call(write_out, out_shape=(jax.ShapeDtypeStruct((samples, width...  2.06 us

profile of v4, /device:TPU:8, one launch (start us, length us, event | category | flops | bytes accessed | tf_op | source)
XLA Modules:
  0.0 78.0 jit_solution(9217355520493312869)
XLA Ops:
  0.6 75.3 %shard_map.146 = (bf16[256,256]{1,0:T(8,128)(2,1)S(1)}, bf16[8,8,32,256]{3,2,1,0:T(8,128)(2,1)S(1)}, f32[8,2,256]{2,1,0:T(2,128)S(1)}) custom-call(bf16[256,256]{1,0:T(8,128)(2,1)} %bitcast.15, bf16[8,256,256]{2,1,0:T(8,128)(2,1)} %bitcast.14, f32[8,256]{1,0:T(8,128)} %bitcast.16, bf16[4,256]{1,0:T(4,128)(2,1)} %refs_3_.1, f32[1,4]{1,0:T(1,128)} %bitcast.23, ...), custom_call_target="tpu_custom_call" | custom-call | tf_op jit(solution)/shard_map/pallas_call | solution.py:590
  75.9 2.1 %shard_map.147 = (bf16[256,256]{1,0:T(8,128)(2,1)}, f32[8,8,32,256]{3,2,1,0:T(8,128)}, f32[8,256]{1,0:T(8,128)}, f32[4,256]{1,0:T(4,128)}, f32[1,4]{1,0:T(1,128)}) custom-call(bf16[256,256]{1,0:T(8,128)(2,1)S(1)} %get-tuple-element.13.in_ref, bf16[8,8,32,256]{3,2,1,0:T(8,128)(2,1)S(1)} %get-tuple-element.14.w_ref, f32[8,2,256]{2,1,0:T(2,128)S(1)} %get-tuple-element.15.small_ref), custom_call_target="tpu_custom_call" | custom-call | tf_op jit(solution)/shard_map/pallas_call | solution.py:634

commit v5 on v4

--- a/solution.py
+++ b/solution.py
@@ -122,6 +122,8 @@
     part,
     chain_send,
     chain_recv,
+    extra_send,
+    extra_recv,
     head_part,
     head_recv,
     small,
@@ -130,6 +132,8 @@
     a2a_recv_sem,
     chain_send_sem,
     chain_recv_sem,
+    extra_send_sem,
+    extra_recv_sem,
     ring_send_sem,
     ring_recv_sem,
     head_send_sem,
@@ -149,8 +153,10 @@
     below = lax.rem(me_d + replicas - 1, replicas)
     most = replicas // 2
 
-    def reach(way, layer):
-        return most - (layer + way) % 2
+    length = most - 1
+
+    def beyond(layer):
+        return lax.rem(me_d + replicas - 2 + 4 * (layer % 2), replicas)
 
     stages = factors(experts)
 
@@ -318,6 +324,16 @@
             device_id_type=MESH,
         )
 
+    def extra_copy(layer):
+        return pltpu.make_async_remote_copy(
+            src_ref=extra_send.at[layer],
+            dst_ref=extra_recv.at[layer],
+            send_sem=extra_send_sem.at[0],
+            recv_sem=extra_recv_sem.at[0, layer],
+            device_id={"dp": beyond(layer)},
+            device_id_type=MESH,
+        )
+
     def shard_of(way, distance):
         if way == 0:
             return lax.rem(me_d + replicas - distance, replicas)
@@ -329,31 +345,30 @@
         small[lax.rem(layer, replicas), pl.ds(layer // replicas, 1), :] = upstream.astype(F32).sum(
             axis=0, keepdims=True
         )
+        extra_send[layer] = part[layer, lax.rem(me_d + most, replicas)].astype(BF16)
+        extra_copy(layer).start()
         for way in range(2):
-            chain_send[way, layer] = part[layer, shard_of(way, reach(way, layer))].astype(BF16)
+            chain_send[way, layer] = part[layer, shard_of(way, length)].astype(BF16)
             chain_copy(way, layer, 0).start()
 
-    def hop(step, layer, way):
+    def hop(step, layer, way, odd):
         chain_copy(way, layer, step - 1).wait_recv()
-        chain_send[way, step * layers + layer] = (
+        total = (
             chain_recv[way, step - 1, layer].astype(F32)
-            + part[layer, shard_of(way, reach(way, layer) - step)]
-        ).astype(BF16)
+            + part[layer, shard_of(way, length - step)]
+        )
+        if step == 1 and way == odd:
+            extra_copy(layer).wait_recv()
+            total = total + extra_recv[layer].astype(F32)
+        chain_send[way, step * layers + layer] = total.astype(BF16)
         chain_copy(way, layer, step).start()
 
     lag = 3
-
-    def hops(i, count):
-        for step in range(1, most - 1):
-            if step <= count:
-                for way in range(2):
-                    pass
 
     def backward_with(count):
         def backward(i, c):
             layer = layers - 1 - i
             weight_grad(layer)
-            hops(i, count)
             spread = matmul(acts[layers], w_ref[layer], ((1,), (1,)))
             acts[layers] = (spread * one_minus_exp(acts[layer].astype(F32))).astype(BF16)
             return c
@@ -374,9 +389,8 @@
     back_send[...] = spread.reshape(experts, cap, width).astype(BF16)
     back_recv[me_e] = back_send[me_e]
     weight_grad(0)
-    hops(layers - 1, 2)
-
-    work = sum(layers for step in range(1, most - 1)) + layers
+
+    work = length * layers // 2
     per_slot = pl.cdiv(experts - 1, work)
 
     def feed(slot):
@@ -398,22 +412,14 @@
         lax.fori_loop(0, layers // 2, pair, 0)
 
     slot = 0
-    for step in range(1, most - 1):
-
-        def remaining(i, c):
+    for step in range(1, length):
+
+        def each(layer, odd):
             for way in range(2):
-                hop(step, layers - 1 - i, way)
-            feed(slot + i)
-            return c
-
-        begin = 0
-        lax.fori_loop(begin, layers, remaining, 0)
-        slot += layers - begin
-
-    def last_hop(layer, odd):
-        for way in range(2):
-            if most - 1 < reach(way, odd):
-                hop(most - 1, layer, way)
+                hop(step, layer, way, odd)
+
+        by_pairs(each, slot)
+        slot += layers // 2
 
     if len(stages) > 2:
         head_finish(2)
@@ -438,9 +444,6 @@
 
     lax.fori_loop(1, replicas, small_start, 0)
 
-    if most > 1:
-        by_pairs(last_hop, slot)
-        slot += layers // 2
 
     def ring_copy(way, layer, step):
         owner = shard_of(1 - way, step)
@@ -453,6 +456,17 @@
             device_id_type=MESH,
         )
 
+    def extra_ring(layer):
+        owner = lax.rem(me_d + replicas + 2 - 4 * (layer % 2), replicas)
+        return pltpu.make_async_remote_copy(
+            src_ref=out_w.at[owner, layer],
+            dst_ref=out_w.at[owner, layer],
+            send_sem=extra_send_sem.at[1],
+            recv_sem=extra_recv_sem.at[1, layer],
+            device_id={"dp": beyond(layer)},
+            device_id_type=MESH,
+        )
+
     def ring_arrive(way, layer, step):
         owner = shard_of(1 - way, step + 1)
         pltpu.make_async_copy(
@@ -462,8 +476,8 @@
     def finish(layer, odd):
         total = part[layer, me_d]
         for way in range(2):
-            chain_copy(way, layer, reach(way, odd) - 1).wait_recv()
-            total = total + chain_recv[way, reach(way, odd) - 1, layer].astype(F32)
+            chain_copy(way, layer, length - 1).wait_recv()
+            total = total + chain_recv[way, length - 1, layer].astype(F32)
         out_w[me_d, layer] = total.astype(BF16)
         for way in range(2):
             ring_copy(way, layer, 0).start()
@@ -490,13 +504,14 @@
 
     lax.fori_loop(1, replicas, small_spread, 0)
 
-    for step in range(1, most):
+    for step in range(1, length):
 
         def forward_on(layer, odd):
             for way in range(2):
-                if step < reach(way, odd):
-                    ring_arrive(way, layer, step - 1)
-                    ring_copy(way, layer, step).start()
+                ring_arrive(way, layer, step - 1)
+                ring_copy(way, layer, step).start()
+                if step == length - 1 and way == odd:
+                    extra_ring(layer).start()
 
         by_pairs(forward_on)
 
@@ -509,7 +524,11 @@
 
     def last(layer, odd):
         for way in range(2):
-            ring_arrive(way, layer, reach(way, odd) - 1)
+            ring_arrive(way, layer, length - 1)
+        owner = lax.rem(me_d + most, replicas)
+        pltpu.make_async_copy(
+            out_w.at[owner, layer], out_w.at[owner, layer], extra_recv_sem.at[1, layer]
+        ).wait()
 
     by_pairs(last)
 
@@ -520,7 +539,8 @@
     for n in range(2):
         pltpu.make_async_copy(peers_d, peers_d, small_send_sem.at[n]).wait()
     for way in range(2):
-        gone = chain_send.at[way, pl.ds(0, most * layers - layers // 2)]
+        pltpu.make_async_copy(extra_send, extra_send, extra_send_sem.at[way]).wait()
+        gone = chain_send.at[way, pl.ds(0, length * layers)]
         pltpu.make_async_copy(gone, gone, chain_send_sem.at[way]).wait()
         pltpu.make_async_copy(gone, gone, ring_send_sem.at[way]).wait()
 
@@ -570,7 +590,8 @@
     cap = 2 * samples // experts
     cells = experts * cap
     piece = width // replicas
-    steps = replicas // 2
+    steps = replicas // 2 - 1
+    assert replicas == 8
     lanes = 128
     dma = pltpu.SemaphoreType.DMA
     operands = (
@@ -612,6 +633,8 @@
             pltpu.VMEM((layers, replicas, piece, width), F32),
             pltpu.VMEM((2, steps * layers, piece, width), BF16),
             pltpu.VMEM((2, steps, layers, piece, width), BF16),
+            pltpu.VMEM((layers, piece, width), BF16),
+            pltpu.VMEM((layers, piece, width), BF16),
             pltpu.VMEM((8, width), F32),
             pltpu.VMEM((3, 8, 8, width), F32),
             pltpu.VMEM((replicas, (layers + 8) // replicas, width), F32),
@@ -620,6 +643,8 @@
             dma((4,)),
             dma((2,)),
             dma((2, steps, layers)),
+            dma((2,)),
+            dma((2, layers)),
             dma((2,)),
             dma((2, steps, layers)),
             dma((3,)),

time: 78.1 us -> 74.5 us (0.954)
  Pallas kernels: 77.3 us -> 73.8 us
    pallas_call x1, Pallas kernels: 75.3 us -> 71.7 us  [per_device(): pl.pallas_call(functools.partial(body, replicas, experts), out_shape=(jax...]
where the time goes in v5:
time: 74.5 us; the launch traced here: 74.4 us
  Pallas kernels  73.8 us (99%)
    pallas_call x1, Pallas kernels, per_device(): pl.pallas_call(functools.partial(body, replicas, experts), out_shape=(jax...  71.7 us
    pallas_call x1, Pallas kernels, per_device(): pl.pallas_call(write_out, out_shape=(jax.ShapeDtypeStruct((samples, width...  2.06 us

profile of v5, /device:TPU:8, one launch (start us, length us, event | category | flops | bytes accessed | tf_op | source)
XLA Modules:
  0.0 74.4 jit_solution(5018321145864239355)
XLA Ops:
  0.6 71.7 %shard_map.146 = (bf16[256,256]{1,0:T(8,128)(2,1)S(1)}, bf16[8,8,32,256]{3,2,1,0:T(8,128)(2,1)S(1)}, f32[8,2,256]{2,1,0:T(2,128)S(1)}) custom-call(bf16[256,256]{1,0:T(8,128)(2,1)} %bitcast.15, bf16[8,256,256]{2,1,0:T(8,128)(2,1)} %bitcast.14, f32[8,256]{1,0:T(8,128)} %bitcast.16, bf16[4,256]{1,0:T(4,128)(2,1)} %refs_3_.1, f32[1,4]{1,0:T(1,128)} %bitcast.23, ...), custom_call_target="tpu_custom_call" | custom-call | tf_op jit(solution)/shard_map/pallas_call | solution.py:611
  72.3 2.1 %shard_map.147 = (bf16[256,256]{1,0:T(8,128)(2,1)}, f32[8,8,32,256]{3,2,1,0:T(8,128)}, f32[8,256]{1,0:T(8,128)}, f32[4,256]{1,0:T(4,128)}, f32[1,4]{1,0:T(1,128)}) custom-call(bf16[256,256]{1,0:T(8,128)(2,1)S(1)} %get-tuple-element.13.in_ref, bf16[8,8,32,256]{3,2,1,0:T(8,128)(2,1)S(1)} %get-tuple-element.14.w_ref, f32[8,2,256]{2,1,0:T(2,128)S(1)} %get-tuple-element.15.small_ref), custom_call_target="tpu_custom_call" | custom-call | tf_op jit(solution)/shard_map/pallas_call | solution.py:659
